TPU v7x, 512 devices: a whole 4x4x16 slice. The times are simulated.
512 devices in a mesh: section: 64 (over y, z), tp: 8 (over x, core).
Axes of the slice: x: 4, y: 4, z: 16, core: 2. Of those that a mesh axis runs over, the one named last changes fastest.
Arguments:
- preview: bfloat16 [1024, 8192], P('section', 'tp'), may hold values from -6 to 6
- row_owner: int32 [1024], P('section'), may hold values from 0 to 31, never falling along the last dimension, each value on 1 to 128 neighbouring positions
- norm_gain: float32 [8192], P('tp'), may hold values from 0.25 to 1.75
- w_gate: bfloat16 [28672, 8192], P('section', 'tp'), may hold values from -0.0625 to 0.0625
- w_up: bfloat16 [28672, 8192], P('section', 'tp'), may hold values from -0.0625 to 0.0625
- w_down: bfloat16 [28672, 8192], P('section', 'tp'), may hold values from -0.03125 to 0.03125
- score_vec: float32 [8192], P('tp'), may hold values from -0.75 to 0.75
Outputs:
- verified: bfloat16 [1024, 8192], P('section', 'tp')
- scores: float32 [32], replicated
Inputs may be any that keep to these rules, and one draw needn't show every extreme that they name: row_owner never falls along the rows; every candidate owns 1 to 128 consecutive rows, some candidate exactly 128.
All inputs are finite; a program needn't handle non-finite values.
Results may differ from a plain program's by a relative error of at most 0.017.
Values may be sent and summed in bfloat16 or wider, within the bound.
A program may use at most 64 MiB of HBM per device.

v0:
```python
import jax
import jax.numpy as jnp
from jax import lax
from jax.sharding import PartitionSpec as P

D = 8192
CAND = 32


def shards(preview, row_owner, norm_gain, w_gate, w_up, w_down, score_vec):
    resid = preview.astype(jnp.float32)
    sq_sum = lax.psum(jnp.sum(resid * resid, axis=1), "tp")
    normed = (resid * lax.rsqrt(sq_sum[:, None] / D + 1e-05) * norm_gain[None, :]).astype(
        jnp.bfloat16
    )
    dims = (((1,), (1,)), ((), ()))
    hidden_cols = w_gate.shape[0]
    piece = lax.all_gather(normed, "section", axis=0, tiled=True)
    gate_part = lax.dot_general(piece, w_gate, dims, preferred_element_type=jnp.float32)
    up_part = lax.dot_general(piece, w_up, dims, preferred_element_type=jnp.float32)
    partial_gu = jnp.concatenate([gate_part, up_part], axis=1)
    summed = lax.psum(partial_gu.astype(jnp.bfloat16), "tp").astype(jnp.float32)
    hidden = (jax.nn.silu(summed[:, :hidden_cols]) * summed[:, hidden_cols:]).astype(jnp.bfloat16)
    own_rows = resid.shape[0]
    full_down = jnp.dot(hidden, w_down, preferred_element_type=jnp.float32)
    total_down = lax.psum(full_down, "section")
    mine = lax.dynamic_slice_in_dim(total_down, lax.axis_index("section") * own_rows, own_rows, 0)
    verified = (resid + mine).astype(jnp.bfloat16)
    row_score = jnp.dot(verified.astype(jnp.float32), score_vec, precision=lax.Precision.HIGHEST)
    member = (row_owner[None, :] == jnp.arange(CAND, dtype=jnp.int32)[:, None]).astype(jnp.float32)
    totals = jnp.dot(member, row_score, precision=lax.Precision.HIGHEST)
    counts = jnp.sum(member, axis=1) / lax.axis_size("tp")
    totals, counts = lax.psum((totals, counts), ("section", "tp"))
    return (verified, totals / counts)


def solution(mesh):
    placed = (
        P("section", "tp"),
        P("section"),
        P("tp"),
        P("section", "tp"),
        P("section", "tp"),
        P("section", "tp"),
        P("tp"),
    )
    return jax.shard_map(
        shards, mesh=mesh, in_specs=placed, out_specs=(P("section", "tp"), P()), check_vma=False
    )
```

profile of v0, /device:TPU:1, one launch (start us, length us, event | category | flops | bytes accessed | tf_op | source)
XLA Modules:
  0.0 653.8 jit_solution(13187137701598601009)
XLA Ops:
  7.2 0.0 copy-start
  7.2 0.0 all-gather.2.cloned.1.call-start
  7.2 0.9 fusion.4
  8.2 18.6 %psum.35 = f32[16]{0:T(128)S(1)} all-reduce(f32[16]{0:T(128)S(1)} %fusion.4), channel_id=1, replica_groups=mesh['section'=64,'tp'=8] {'tp'}, use_global_device_ids=true, to_apply=%region_1.0 | all-reduce | flops 16 | bytes 128 | tf_op jit(solution)/shard_map/psum | solution.py:12
  26.8 1.5 fusion.6
  28.3 0.0 all-gather.2.cloned.1.call-update
  28.3 0.0 copy-start.4
  28.3 0.0 all-reduce.4.cloned.1.call-start
  28.4 131.0 %all-gather.2.cloned.1.call-done = bf16[1024,1024]{1,0:T(8,128)(2,1)} async-done(((bf16[16,1024]{1,0:T(8,128)(2,1)}), bf16[1024,1024]{1,0:T(8,128)(2,1)}) %all-gather.2.cloned.1.call-update) | async-done | bytes 2097168 | tf_op jit(solution)/shard_map/all_gather | solution.py:18
  159.4 3.1 convolution_convert_fusion
  162.5 0.0 copy-done.4
  162.5 0.0 copy-done.3
  162.5 1.2 convolution_convert_fusion.1
  163.7 1.4 pad_maximum_fusion
  165.1 0.0 all-reduce.4.cloned.1.call-update
  165.1 0.0 all-reduce.6.cloned.1.call-start
  165.2 83.4 %all-reduce.4.cloned.1.call-done = bf16[1024,896]{0,1:T(8,128)(2,1)} async-done(((bf16[1024,896]{0,1:T(8,128)(2,1)}), bf16[1024,896]{0,1:T(8,128)(2,1)}) %all-reduce.4.cloned.1.call-update) | async-done | bytes 1835024 | tf_op jit(solution)/shard_map/psum | solution.py:22
  248.6 1.9 convert_element_type.22
  250.5 0.0 copy-done
  250.5 3.3 fusion.1
  253.8 0.0 all-reduce.6.cloned.1.call-update
  253.9 0.6 copy-done.6
  254.5 0.1 convert_reduce_fusion
  254.6 281.4 %all-reduce.6.cloned.1.call-done = f32[1024,1024]{1,0:T(8,128)} async-done(((f32[1024,1024]{1,0:T(8,128)}), f32[1024,1024]{1,0:T(8,128)}) %all-reduce.6.cloned.1.call-update) | async-done | bytes 4194320 | tf_op jit(solution)/shard_map/psum | solution.py:26
  536.0 0.0 copy-done.1
  536.0 0.8 fusion.7
  536.8 0.0 copy-start.2
  536.8 0.0 copy-done.5
  536.8 0.1 convolution_bitcast_fusion.1
  537.0 0.2 convolution_bitcast_fusion
  537.2 109.5 %all-reduce = (f32[32]{0:T(128)S(1)}, f32[32]{0:T(128)S(1)}) all-reduce(f32[32]{0:T(128)S(1)} %convolution_bitcast_fusion, f32[32]{0:T(128)S(1)} %broadcast_multiply_fusion), channel_id=1, replica_groups=mesh['section'=64,'tp'=8] {'section','tp'}, use_global_device_ids=true, to_apply=%region_4.5 | all-reduce | flops 64 | bytes 512 | tf_op jit(solution)/shard_map/psum | solution.py:33
  646.7 0.5 div.20
  (7 shorter events, 0.0 us)
Async XLA Ops:
  7.2 243.3 %copy-start = (bf16[448,1024]{1,0:T(8,128)(2,1)S(1)}, bf16[448,1024]{1,0:T(8,128)(2,1)}, u32[]{:S(2)}) copy-start(bf16[448,1024]{1,0:T(8,128)(2,1)} %param.12) | copy-start | bytes 2752516
  7.2 152.2 %all-gather.2.cloned.1.call-start = ((), (), s32[]{:S(2)}) async-start(), calls=%async_computation | async-start | bytes 2129920 | tf_op jit(solution)/shard_map/all_gather | solution.py:18
  28.3 134.2 %copy-start.4 = (bf16[448,1024]{1,0:T(8,128)(2,1)S(1)}, bf16[448,1024]{1,0:T(8,128)(2,1)}, u32[]{:S(2)}) copy-start(bf16[448,1024]{1,0:T(8,128)(2,1)} %param.10) | copy-start | bytes 2752516
  28.3 220.3 %all-reduce.4.cloned.1.call-start = ((), (), s32[]{:S(2)}) async-start(), calls=%async_computation.1 | async-start | bytes 3670016 | tf_op jit(solution)/shard_map/psum | solution.py:22
  159.4 3.1 copy-start.3
  165.1 370.8 %all-reduce.6.cloned.1.call-start = ((), (), s32[]{:S(2)}) async-start(), calls=%async_computation.2 | async-start | bytes 8388608 | tf_op jit(solution)/shard_map/psum | solution.py:26
  253.8 0.7 copy-start.6
  253.8 282.1 %copy-start.1 = (bf16[16,1024]{1,0:T(8,128)(2,1)S(1)}, bf16[16,1024]{1,0:T(8,128)(2,1)}, u32[]{:S(2)}) copy-start(bf16[16,1024]{1,0:T(8,128)(2,1)} %param.7) | copy-start | bytes 98308
  253.8 283.0 %copy-start.5 = (f32[1024]{0:T(1024)S(1)}, f32[1024]{0:T(1024)}, u32[]{:S(2)}) copy-start(f32[1024]{0:T(1024)} %param.13) | copy-start | bytes 12292
  536.8 110.4 %copy-start.2 = (bf16[16,1024]{1,0:T(8,128)(2,1)}, bf16[16,1024]{1,0:T(8,128)(2,1)S(1)}, u32[]{:S(2)}) copy-start(bf16[16,1024]{1,0:T(8,128)(2,1)S(1)} %fusion.7) | copy-start | bytes 98308
Sparse Core Ops, SparseCore 0:
  28.4 130.9 all-gather.1
  165.2 83.3 all-reduce.3
  254.0 281.9 all-reduce.5
where the time goes:
time: 654 us
  waiting for transfers between devices  496 us (76%)
  blocking collectives  128 us (20%)
  between operations  13.8 us (2%)
  matrix products  7.94 us (1%)
  other arithmetic  7.13 us (1%)
    psum x1, waiting for transfers between devices, shards(): total_down = lax.psum(full_down, 'section')  281 us
    all_gather x1, waiting for transfers between devices, shards(): piece = lax.all_gather(normed, 'section', axis=0, tiled=True)  131 us
    psum x1, blocking collectives, shards(): totals, counts = lax.psum((totals, counts), ('section', 'tp'))  110 us
    psum x1, waiting for transfers between devices, shards(): summed = lax.psum(partial_gu.astype(jnp.bfloat16), 'tp').astype(jnp.float32)  83.4 us
    psum x1, blocking collectives, shards(): sq_sum = lax.psum(jnp.sum(resid * resid, axis=1), 'tp')  18.6 us
  transfers between devices with their start and end apart: 3, of which 3 were waited for; matrix products, arithmetic and copies ran while one was open for 0% of the time, Pallas kernels for 0%

commit v1 on v0

v1 whole, which is shorter than its diff:
```python
import functools

import jax
import jax.numpy as jnp
from jax import lax
from jax.experimental import pallas as pl
from jax.experimental.pallas import tpu as pltpu
from jax.sharding import PartitionSpec as P

CAND = 32
NY = 4
NX = 4
EPS = 1e-05
BF = jnp.bfloat16
F32 = jnp.float32


class Plan:
    def __init__(self, nz, rows, feats, hidden, groups):
        self.nz, self.hz = nz, nz // 2
        self.rows, self.feats, self.hidden = rows, feats, hidden
        self.ng, self.q = groups, nz // groups
        self.half = self.q // 2 * NY * rows
        self.blk = self.half // NX
        self.hpad = -(-hidden // 128) * 128
        self.full = hidden // 128 * 128
        self.rest = hidden - self.full
        tiles = feats // 128
        self.wa = max(1, (tiles * 3) // 8) * 128
        self.wb = feats - self.wa
        self.wc = max(1, self.wb // 128 // 2 + (self.wb // 128) % 2) * 128
        if self.wc >= self.wb:
            self.wc = self.wb


def kernel(pn, prev_ref, owner_ref, gain_ref, wg_ref, wu_ref, wd_ref, sv_ref, out_ref, score_ref,
           x, wgu, wd, nrm, gus, guo, rc, rx1, rx2, gux, hid, pt, rza, rzb, ry1, ry2, rya, sc, lsem, ssem, rsem):
    nz, hz = pn.nz, pn.hz
    wa, wb, wc = pn.wa, pn.wb, pn.wc
    A, B = pl.ds(0, wa), pl.ds(wa, wb)
    B1, B2 = pl.ds(wa, wc), pl.ds(wa + wc, wb - wc)
    s, t = lax.axis_index("section"), lax.axis_index("tp")
    yy, zz = s // nz, s % nz
    xx, cc = t // 2, t % 2

    def dev(dx=0, dy=0, dz=0, other=False):
        sec = ((yy + dy) % NY) * nz + (zz + dz) % nz
        core = 1 - cc if other else cc
        return (sec, ((xx + dx) % NX) * 2 + core)

    count = [0]
    flying = []

    def send(src, dst, to):
        i = count[0]
        count[0] += 1
        copy = pltpu.make_async_remote_copy(
            src_ref=src, dst_ref=dst, send_sem=ssem.at[i], recv_sem=rsem.at[i],
            device_id=to, device_id_type=pl.DeviceIdType.MESH)
        copy.start()
        flying.append(copy)
        return copy

    full, rest = pn.full, pn.rest
    loads = []

    def load(src, dst):
        copy = pltpu.make_async_copy(src, dst, lsem.at[len(loads)])
        copy.start()
        loads.append(copy)

    if full:
        load(wg_ref.at[pl.ds(0, full)], wgu.at[pl.ds(0, full)])
        load(wu_ref.at[pl.ds(0, full)], wgu.at[pl.ds(full, full)])
    if rest:
        load(wg_ref.at[pl.ds(full, rest)], wgu.at[pl.ds(2 * full, rest)])
        load(wu_ref.at[pl.ds(full, rest)], wgu.at[pl.ds(2 * full + rest, rest)])
    load(wd_ref, wd.at[pl.ds(0, pn.hidden)])
    if rest:
        wd[pl.ds(pn.hidden, pn.hpad - pn.hidden), :] = jnp.zeros((pn.hpad - pn.hidden, pn.feats), BF)

    tp_peers = [dev(dx=dx, other=o) for dx in range(NX) for o in (False, True) if (dx, o) != (0, False)]
    y_peers = [dev(dy=dy) for dy in range(1, NY)]
    z_peers = [dev(dz=dz) for dz in range(1, nz)]
    barrier = pltpu.get_barrier_semaphore()
    for peer in tp_peers + y_peers + z_peers:
        pl.semaphore_signal(barrier, inc=1, device_id=peer, device_id_type=pl.DeviceIdType.MESH)
    pl.semaphore_wait(barrier, len(tp_peers + y_peers + z_peers))

    own = prev_ref[...].astype(F32)
    sq = jnp.sum(own * own, axis=1, keepdims=True)
    nrm[0] = jnp.broadcast_to(sq, (pn.rows, 128))
    copies = [send(nrm.at[0], nrm.at[i + 1], peer) for i, peer in enumerate(tp_peers)]
    for c in copies:
        c.wait_recv()
    tot = nrm[0]
    for i in range(len(tp_peers)):
        tot = tot + nrm[i + 1]
    rs = lax.rsqrt(tot[:, 0:1] / (pn.feats * NX * 2) + EPS)
    x[0, 0] = (own * rs * gain_ref[...]).astype(BF)

    def pair(k):
        if k == 0:
            return [0]
        return [nz - 1] if k == hz else [2 * k - 1, 2 * k]

    def pslice(k):
        p = pair(k)
        return pl.ds(p[0], len(p))

    def gather():
        za, zb, y1, y2 = {}, {}, {}, {}

        def step_b(k):
            lo, hi = max(2 * k - 3, 0), 2 * k - 2
            if k < hz:
                zb[k] = [send(x.at[lo, 0, :, B], x.at[2 * k - 1, 0, :, B], dev(dz=1)),
                         send(x.at[hi, 0, :, B], x.at[2 * k, 0, :, B], dev(dz=-1))]
            else:
                zb[k] = [send(x.at[lo, 0, :, B1], x.at[nz - 1, 0, :, B1], dev(dz=1))]
                if wc < wb:
                    zb[k].append(send(x.at[hi, 0, :, B2], x.at[nz - 1, 0, :, B2], dev(dz=-1)))

        def step_a(k):
            lo, hi = max(2 * k - 3, 0), 2 * k - 2
            if k < hz:
                za[k] = [send(x.at[lo, :, :, A], x.at[2 * k - 1, :, :, A], dev(dz=1)),
                         send(x.at[hi, :, :, A], x.at[2 * k, :, :, A], dev(dz=-1))]
            else:
                za[k] = [send(x.at[lo, pl.ds(0, 2), :, A], x.at[nz - 1, pl.ds(0, 2), :, A], dev(dz=1)),
                         send(x.at[hi, pl.ds(2, 2), :, A], x.at[nz - 1, pl.ds(2, 2), :, A], dev(dz=-1))]

        def step_y1(k):
            y1[k] = [send(x.at[pslice(k), 0, :, B], x.at[pslice(k), 1, :, B], dev(dy=1)),
                     send(x.at[pslice(k), 0, :, B], x.at[pslice(k), 2, :, B], dev(dy=-1))]

        def step_y2(k):
            for c in y1[k]:
                c.wait_recv()
            y2[k] = []
            for q in pair(k):
                j, dy = (1, 1) if q % 2 else (2, -1)
                y2[k].append(send(x.at[q, j, :, B], x.at[q, 3, :, B], dev(dy=dy)))

        def finish_y2(k):
            for c in y2[k]:
                c.wait_recv()

        first = [send(x.at[0, 0, :, A], x.at[0, 1, :, A], dev(dy=1)),
                 send(x.at[0, 0, :, A], x.at[0, 2, :, A], dev(dy=-1)),
                 send(x.at[0, 0, :, A], x.at[0, 3, :, A], dev(dy=2))]
        step_b(1)
        step_y1(0)
        for c in first:
            c.wait_recv()
        step_a(1)
        for k in range(1, hz + 3):
            if k <= hz:
                for c in zb[k]:
                    c.wait_recv()
                if k < hz:
                    step_b(k + 1)
                step_y1(k)
                for c in za[k]:
                    c.wait_recv()
                if k < hz:
                    step_a(k + 1)
            if k - 1 <= hz:
                step_y2(k - 1)
            if k >= 2:
                finish_y2(k - 2)
                yield k - 2

    dims = (((1,), (1,)), ((), ()))
    hq = pn.q // 2
    half, blk = pn.half, pn.blk

    def product(q0):
        rows = x[pl.ds(q0, hq)].reshape(half, pn.feats)
        return lax.dot_general(rows, wgu[...], dims, preferred_element_type=F32)

    def group(g):
        other, mine = g * pn.q + (1 - cc) * hq, g * pn.q + cc * hq
        gus[g] = product(other).astype(BF)
        c1 = send(gus.at[g], rc.at[g], dev(other=True))
        guo[g] = product(mine)
        yield
        c1.wait_recv()
        guo[g] = guo[g] + rc[g].astype(F32)

        def at(dx, start=0):
            return pl.multiple_of(((xx + dx) % NX) * blk, blk) + start

        hb = blk // 2
        gux[g, 2] = guo[g, pl.ds(at(2), blk)].astype(BF)
        x1 = [send(gux.at[g, 2, pl.ds(0, hb)], rx1.at[g, 0], dev(dx=1)),
              send(gux.at[g, 2, pl.ds(hb, hb)], rx1.at[g, 1], dev(dx=-1))]
        yield
        for c in x1:
            c.wait_recv()
        gux[g, 0, pl.ds(0, hb)] = (guo[g, pl.ds(at(1), hb)] + rx1[g, 0].astype(F32)).astype(BF)
        gux[g, 0, pl.ds(hb, hb)] = guo[g, pl.ds(at(1, hb), hb)].astype(BF)
        gux[g, 1, pl.ds(0, hb)] = guo[g, pl.ds(at(-1), hb)].astype(BF)
        gux[g, 1, pl.ds(hb, hb)] = (guo[g, pl.ds(at(-1, hb), hb)] + rx1[g, 1].astype(F32)).astype(BF)
        x2 = [send(gux.at[g, 0], rx2.at[g, 0], dev(dx=1)),
              send(gux.at[g, 1], rx2.at[g, 1], dev(dx=-1))]
        yield
        for c in x2:
            c.wait_recv()
        gu = guo[g, pl.ds(at(0), blk)] + rx2[g, 0].astype(F32) + rx2[g, 1].astype(F32)

        def act(gate, up):
            return (gate / (1.0 + jnp.exp(-gate)) * up).astype(BF)

        if full:
            hid[g, cc, xx, :, pl.ds(0, full)] = act(gu[:, 0:full], gu[:, full:2 * full])
        if rest:
            last = gu[:, 2 * full:]
            lane = lax.broadcasted_iota(jnp.int32, last.shape, 1)
            value = act(last, pltpu.roll(last, 128 - rest, 1))
            hid[g, cc, xx, :, pl.ds(full, 128)] = jnp.where(lane < rest, value, jnp.zeros_like(value))
        own_h = hid.at[g, cc, xx]
        h1 = [send(own_h, own_h, dev(dx=1)), send(own_h, own_h, dev(dx=-1))]
        yield
        for c in h1:
            c.wait_recv()
        left = hid.at[g, cc, (xx + NX - 1) % NX, pl.ds(0, hb)]
        right = hid.at[g, cc, (xx + 1) % NX, pl.ds(hb, hb)]
        h2 = [send(left, left, dev(dx=1)), send(right, right, dev(dx=-1))]
        yield
        for c in h2:
            c.wait_recv()
        c2 = send(hid.at[g, cc], hid.at[g, cc], dev(other=True))
        yield
        c2.wait_recv()
        rows = hid[g].reshape(2 * half, pn.hpad)
        down = jnp.dot(rows, wd[...], preferred_element_type=F32)
        pt[pl.ds(g * pn.q, pn.q)] = down.astype(BF).reshape(pn.q, NY, pn.rows, pn.feats)

    waiting = list(range(pn.ng))
    active = []
    loaded = [False]

    def advance():
        for gen in list(active):
            try:
                next(gen)
            except StopIteration:
                active.remove(gen)

    for done in gather():
        advance()
        if waiting and done >= ((waiting[0] + 1) * pn.q) // 2:
            if not loaded[0]:
                for c in loads:
                    c.wait()
                loaded[0] = True
            gen = group(waiting.pop(0))
            next(gen)
            active.append(gen)
    while active:
        advance()

    def add(dst, *terms):
        v = dst[...].astype(F32)
        for term in terms:
            v = v + term.astype(F32)
        dst[...] = v.astype(BF)

    za, zb, y1, y2 = {}, {}, {}, {}

    def rs_a(m):
        if m == hz:
            q = nz - 1
            za[m] = [send(pt.at[q, pl.ds(0, 2), :, A], rza.at[m - 1, 0, pl.ds(0, 2)], dev(dz=1)),
                     send(pt.at[q, pl.ds(2, 2), :, A], rza.at[m - 1, 1, pl.ds(2, 2)], dev(dz=-1))]
            return
        for c in za[m + 1]:
            c.wait_recv()
        for d, q in ((0, 2 * m), (1, 2 * m - 1)):
            js = pl.ds(0, NY) if m + 1 < hz else pl.ds(2 * d, 2)
            add(pt.at[q, js, :, A], rza[m, d, js])
        za[m] = [send(pt.at[2 * m, :, :, A], rza.at[m - 1, 0], dev(dz=1)),
                 send(pt.at[2 * m - 1, :, :, A], rza.at[m - 1, 1], dev(dz=-1))]

    def part(m, d):
        if m < hz:
            return B, pl.ds(0, wb)
        return (B1, pl.ds(0, wc)) if d == 0 else (B2, pl.ds(wc, wb - wc))

    def rs_b(m):
        if m < hz:
            for c in zb[m + 1]:
                c.wait_recv()
            for d, q in ((0, 2 * m), (1, 2 * m - 1)):
                cols, rcols = part(m + 1, d)
                if cols.size:
                    add(pt.at[q, 0, :, cols], rzb[m, d, :, rcols])
        zb[m] = []
        for d, dz in ((0, 1), (1, -1)):
            q = nz - 1 if m == hz else 2 * m - d
            cols, rcols = part(m, d)
            if cols.size:
                zb[m].append(send(pt.at[q, 0, :, cols], rzb.at[m - 1, d, :, rcols], dev(dz=dz)))

    def rs_y1(m):
        y1[m] = [send(pt.at[q, 3, :, B], ry1.at[q], dev(dy=1 if q % 2 else -1)) for q in pair(m)]

    def rs_y2(m):
        for c in y1[m]:
            c.wait_recv()
        for q in pair(m):
            add(pt.at[q, 2 if q % 2 else 1, :, B], ry1[q])
        y2[m] = [send(pt.at[pslice(m), 2, :, B], ry2.at[0, pslice(m)], dev(dy=1)),
                 send(pt.at[pslice(m), 1, :, B], ry2.at[1, pslice(m)], dev(dy=-1))]

    def rs_y3(m):
        for c in y2[m]:
            c.wait_recv()
        for q in pair(m):
            add(pt.at[q, 0, :, B], ry2[0, q], ry2[1, q])

    fin = []
    for i in range(hz + 3):
        m = hz - i
        if m >= 0:
            rs_y1(m)
        if m >= 1:
            rs_a(m)
        if m == 0:
            for c in za[1]:
                c.wait_recv()
            add(pt.at[0, :, :, A], rza[0, 0], rza[0, 1])
            fin = [send(pt.at[0, 1, :, A], rya.at[0], dev(dy=-1)),
                   send(pt.at[0, 2, :, A], rya.at[1], dev(dy=1)),
                   send(pt.at[0, 3, :, A], rya.at[2], dev(dy=2))]
        if 0 <= m + 1 <= hz:
            rs_y2(m + 1)
        if 0 <= m + 2 <= hz:
            rs_y3(m + 2)
            if m + 2 >= 1:
                rs_b(m + 2)
    for c in fin:
        c.wait_recv()
    va = pt[0, 0, :, A].astype(F32)
    for i in range(3):
        va = va + rya[i].astype(F32)
    va = (va + prev_ref[:, A].astype(F32)).astype(BF)
    out_ref[:, A] = va
    for c in zb[1]:
        c.wait_recv()
    vb = pt[0, 0, :, B].astype(F32) + rzb[0, 0].astype(F32) + rzb[0, 1].astype(F32)
    vb = (vb + prev_ref[:, B].astype(F32)).astype(BF)
    out_ref[:, B] = vb

    row = (jnp.sum(va.astype(F32) * sv_ref[:, A], axis=1, keepdims=True)
           + jnp.sum(vb.astype(F32) * sv_ref[:, B], axis=1, keepdims=True))
    lane = lax.broadcasted_iota(jnp.int32, (1, 128), 1)
    total = jnp.zeros((1, 128), F32)
    number = jnp.zeros((1, 128), F32)
    for r in range(pn.rows):
        hit = lane == owner_ref[r]
        total = total + jnp.where(hit, row[r:r + 1, :], 0.0)
        number = number + jnp.where(hit, 1.0, 0.0)
    sub = lax.broadcasted_iota(jnp.int32, (8, 128), 0)
    acc = jnp.where(sub == 0, total, jnp.where(sub == 1, number, 0.0))
    base = 0
    for peers in (tp_peers, y_peers, z_peers):
        sc[base] = acc
        copies = [send(sc.at[base], sc.at[base + 1 + i], peer) for i, peer in enumerate(peers)]
        for i, c in enumerate(copies):
            c.wait_recv()
            acc = acc + sc[base + 1 + i]
        base += 1 + len(peers)
    score_ref[...] = acc[0:1, :] / jnp.maximum(acc[1:2, :] / (NX * 2), 1e-30)
    for c in flying:
        c.wait_send()


def shards(nz, groups, preview, row_owner, norm_gain, w_gate, w_up, w_down, score_vec):
    rows, feats = preview.shape
    hidden = w_gate.shape[0]
    pn = Plan(nz, rows, feats, hidden, groups)
    ng, half, blk = pn.ng, pn.half, pn.blk
    width = 2 * hidden
    sems = 600
    vmem = pl.BlockSpec(memory_space=pltpu.VMEM)
    hbm = pl.BlockSpec(memory_space=pl.ANY)
    verified, scores = pl.pallas_call(
        functools.partial(kernel, pn),
        out_shape=(jax.ShapeDtypeStruct((rows, feats), BF), jax.ShapeDtypeStruct((1, 128), F32)),
        in_specs=[vmem, pl.BlockSpec(memory_space=pltpu.SMEM), vmem, hbm, hbm, hbm, vmem],
        out_specs=(vmem, vmem),
        scratch_shapes=[
            pltpu.VMEM((nz, NY, rows, feats), BF),
            pltpu.VMEM((width, feats), BF),
            pltpu.VMEM((pn.hpad, feats), BF),
            pltpu.VMEM((2 * NX, rows, 128), F32),
            pltpu.VMEM((ng, half, width), BF),
            pltpu.VMEM((ng, half, width), F32),
            pltpu.VMEM((ng, half, width), BF),
            pltpu.VMEM((ng, 2, blk // 2, width), BF),
            pltpu.VMEM((ng, 2, blk, width), BF),
            pltpu.VMEM((ng, 3, blk, width), BF),
            pltpu.VMEM((ng, 2, NX, blk, pn.hpad), BF),
            pltpu.VMEM((nz, NY, rows, feats), BF),
            pltpu.VMEM((pn.hz, 2, NY, rows, pn.wa), BF),
            pltpu.VMEM((pn.hz, 2, rows, pn.wb), BF),
            pltpu.VMEM((nz, rows, pn.wb), BF),
            pltpu.VMEM((2, nz, rows, pn.wb), BF),
            pltpu.VMEM((3, rows, pn.wa), BF),
            pltpu.VMEM((2 * NX + NY + nz, 8, 128), F32),
            pltpu.SemaphoreType.DMA((5,)),
            pltpu.SemaphoreType.DMA((sems,)),
            pltpu.SemaphoreType.DMA((sems,)),
        ],
        compiler_params=pltpu.CompilerParams(
            collective_id=0, has_side_effects=True, vmem_limit_bytes=56 << 20),
    )(preview, row_owner, norm_gain[None, :], w_gate, w_up, w_down, score_vec[None, :])
    return verified, scores[0, :CAND]


def solution(mesh):
    placed = (
        P("section", "tp"),
        P("section"),
        P("tp"),
        P("section", "tp"),
        P("section", "tp"),
        P("section", "tp"),
        P("tp"),
    )
    nz = mesh.shape["section"] // NY
    return jax.shard_map(
        functools.partial(shards, nz, 2), mesh=mesh, in_specs=placed,
        out_specs=(P("section", "tp"), P()), check_vma=False
    )
```

time: 654 us -> 151 us (0.23)
  waiting for transfers between devices: 496 us -> 0 us
  Pallas kernels: 0 us -> 148 us
  blocking collectives: 128 us -> 0 us
  between operations: 13.8 us -> 0.65 us
  matrix products: 7.94 us -> 0 us
  other arithmetic: 7.13 us -> 0 us
    psum x2 -> x0, waiting for transfers between devices: 365 us -> none  [the longest x1 281 us: shards(): total_down = lax.psum(full_down, 'section')]
    pallas_call x0 -> x1, Pallas kernels: none -> 148 us  [shards(): pl.pallas_call(functools.partial(kernel, pn), out_shape=(jax.ShapeDtypeSt...]
    all_gather x1 -> x0, waiting for transfers between devices: 131 us -> none  [shards(): piece = lax.all_gather(normed, 'section', axis=0, tiled=True)]
    psum x2 -> x0, blocking collectives: 128 us -> none  [the longest x1 110 us: shards(): totals, counts = lax.psum((totals, counts), ('section', 'tp'))]
    dot_general x5 -> x0, matrix products: 7.94 us -> none  [the longest x1 3.32 us: shards(): full_down = jnp.dot(hidden, w_down, preferred_element_type=jnp.float32)]
  transfers between devices with their start and end apart: 3 -> 0, of which waited for: 3 -> 0; matrix products, arithmetic and copies ran while one was open for 0% -> 0% of each run, Pallas kernels for 0% -> 0%
where the time goes in v1:
time: 151 us
  Pallas kernels  148 us (98%)
  local copies, waits for them, and re-layouts  2.51 us (2%)
    pallas_call x1, Pallas kernels, shards(): pl.pallas_call(functools.partial(kernel, pn), out_shape=(jax.ShapeDtypeSt...  148 us

profile of v1, /device:TPU:1, one launch (start us, length us, event | category | flops | bytes accessed | tf_op | source)
XLA Modules:
  0.0 150.8 jit_solution(2804923145034345126)
XLA Ops:
  0.6 147.6 %shard_map.86 = (bf16[16,1024]{1,0:T(8,128)(2,1)}, f32[1,128]{1,0:T(1,128)}) custom-call(bf16[16,1024]{1,0:T(8,128)(2,1)} %prev_ref.1, s32[16]{0:T(128)} %owner_ref.1, f32[1,1024]{1,0:T(1,128)} %bitcast.4, bf16[448,1024]{1,0:T(8,128)(2,1)} %wg_ref.1, bf16[448,1024]{1,0:T(8,128)(2,1)} %wu_ref.1, bf16[448,1024]{1,0:T(8,128)(2,1)} %wd_ref.1, f32[1,1024]{1,0:T(1,128)} %bitcast.5), custom_call_target="tpu_custom_call" | custom-call | tf_op jit(solution)/shard_map/pallas_call | solution.py:389
  148.3 0.0 copy-start
  148.3 0.6 copy-done
  148.9 0.5 slice_bitcast_fusion
  149.4 1.4 copy.10
Async XLA Ops:
  148.3 0.6 copy-start

commit v2 on v0

v2 whole, which is shorter than its diff:
```python
import functools

import jax
import jax.numpy as jnp
from jax import lax
from jax.experimental import pallas as pl
from jax.experimental.pallas import tpu as pltpu
from jax.sharding import PartitionSpec as P

CAND = 32
NX, NY, NZ = 4, 4, 16
NW = 4
EPS = 1e-05
BF = jnp.bfloat16
F32 = jnp.float32
FAR = (0, 4, -4, 8)
NT = (((1,), (1,)), ((), ()))
MESH = pl.DeviceIdType.MESH


def split(v, parts):
    out = []
    for _ in range(parts):
        term = v.astype(BF)
        out.append(term)
        v = v - term.astype(F32)
    return out


def stacked(terms, rows):
    width = terms[0].shape[1]
    sub = lax.broadcasted_iota(jnp.int32, (rows, width), 0)
    out = jnp.zeros((rows, width), F32)
    for i, term in enumerate(terms):
        out = jnp.where(sub == i, term.astype(F32), out)
    return out.astype(BF)


def kernel(pa, prev_ref, owner_ref, gain_ref, wg_ref, wu_ref, wd_ref, sv_ref, out_ref, score_ref,
           x, wgu, wt, wd, vv, gus, guo, gub, rc, rx, hid, pt, r1p, r1q, r2p, r2q, fs, rf, ow, rsc, sc,
           lsem, ssem, rsem):
    rows, feats, hidden = prev_ref.shape[0], prev_ref.shape[1], wg_ref.shape[0]
    hpad = -(-hidden // 128) * 128
    full = hidden // 128 * 128
    rest = hidden - full
    width = 2 * hidden
    half, blk = 2 * NY * rows, 2 * NY * rows // NX
    A, B = pl.ds(0, pa), pl.ds(pa, feats - pa)
    s, t = lax.axis_index("section"), lax.axis_index("tp")
    yy, zz = s // NZ, s % NZ
    xx, cc = t // 2, t % 2
    near = (0, -1, 1, 2 * (1 - 2 * (zz % 2)))
    side = (0, -1, 1, 2)

    def dev(dx=0, dy=0, dz=0, other=False):
        core = 1 - cc if other else cc
        return (((yy + dy + NY) % NY) * NZ + (zz + dz + NZ) % NZ, ((xx + dx) % NX) * 2 + core)

    used = [0]
    flying = []

    def send(items, union):
        i = used[0]
        used[0] += 1
        for src, dst, to in items:
            pltpu.make_async_remote_copy(src_ref=src, dst_ref=dst, send_sem=ssem.at[i], recv_sem=rsem.at[i],
                                         device_id=to, device_id_type=MESH).start()
        whole = pltpu.make_async_remote_copy(src_ref=union, dst_ref=union, send_sem=ssem.at[i], recv_sem=rsem.at[i],
                                             device_id=items[0][2], device_id_type=MESH)
        flying.append(whole)
        return whole

    loads = []

    def load(src, dst):
        copy = pltpu.make_async_copy(src, dst, lsem.at[len(loads)])
        copy.start()
        loads.append(copy)

    if full:
        load(wg_ref.at[pl.ds(0, full)], wgu.at[pl.ds(0, full)])
        load(wu_ref.at[pl.ds(0, full)], wgu.at[pl.ds(full, full)])
    if rest:
        load(wg_ref.at[pl.ds(full, rest)], wgu.at[pl.ds(2 * full, rest)])
        load(wu_ref.at[pl.ds(full, rest)], wgu.at[pl.ds(2 * full + rest, rest)])
    load(wd_ref, wd.at[pl.ds(0, hidden)])
    if rest:
        wd[pl.ds(hidden, hpad - hidden), :] = jnp.zeros((hpad - hidden, feats), BF)
    x[0, 0, 0] = prev_ref[...]
    lane = lax.broadcasted_iota(jnp.int32, (1, 128), 1)
    mine = jnp.zeros((1, 128), jnp.int32)
    for r in range(rows):
        mine = jnp.where(lane % rows == r, owner_ref[r], mine)
    ow[0, 0, 0] = mine

    tp_peers = [dev(dx=dx, other=o) for dx in range(NX) for o in (False, True) if (dx, o) != (0, False)]
    y_peers = [dev(dy=dy) for dy in range(1, NY)]
    z_peers = [dev(dz=dz) for dz in range(1, NZ)]
    barrier = pltpu.get_barrier_semaphore()
    for peer in z_peers + y_peers + tp_peers:
        pl.semaphore_signal(barrier, inc=1, device_id=peer, device_id_type=MESH)
    pl.semaphore_wait(barrier, len(tp_peers + y_peers + z_peers))

    got = {}
    tasks = []

    def task(when):
        def add(fn):
            tasks.append((when, len(tasks), fn))
            return fn
        return add

    def spread(w):
        got["p2", w] = send([(x.at[w, 0, 0, :, A], x.at[w, 0, j, :, A], dev(dy=-side[j])) for j in (1, 2, 3)],
                            x.at[w, 0, pl.ds(1, 3), :, A])
        got["q2", w] = send([(x.at[w, 0, 0, :, B], x.at[w, n, 0, :, B], dev(dz=-near[n])) for n in (1, 2, 3)],
                            x.at[w, pl.ds(1, 3), 0, :, B])

    for w in (3, 1, 2):
        got["far", w] = send([(x.at[0, 0, 0], x.at[w, 0, 0], dev(dz=-FAR[w]))], x.at[w, 0, 0])
    spread(0)
    got["o1"] = send([(ow.at[0, 0, 0], ow.at[w, 0, 0], dev(dz=-FAR[w])) for w in (1, 2, 3)], ow.at[pl.ds(1, 3), 0, 0])

    begin = {0: 0.0, 1: 4.8, 2: 4.9, 3: 7.4}
    ready = {0: 8.0, 1: 12.0, 2: 14.0, 3: 16.5}

    for w in range(NW):
        if w:
            @task(begin[w])
            def _(w=w):
                got["far", w].wait_recv()
                spread(w)

        @task(begin[w] + 3.2)
        def _(w=w):
            got["p2", w].wait_recv()
            got["p3", w] = send([(x.at[w, 0, :, :, A], x.at[w, n, :, :, A], dev(dz=-near[n])) for n in (1, 2, 3)],
                                x.at[w, pl.ds(1, 3), :, :, A])

        @task(begin[w] + 3.3)
        def _(w=w):
            got["q2", w].wait_recv()
            got["q3", w] = send([(x.at[w, :, 0, :, B], x.at[w, :, j, :, B], dev(dy=-side[j])) for j in (1, 2, 3)],
                                x.at[w, :, pl.ds(1, 3), :, B])

    step = 128
    for i in range(width // step):
        @task(0.1 + 0.3 * i)
        def _(i=i):
            if i == 0:
                for copy in loads:
                    copy.wait()
            piece = wgu[pl.ds(i * step, step), :].astype(F32) * gain_ref[...]
            wt[:, pl.ds(i * step, step)] = piece.astype(BF).T

    svs = stacked(split(sv_ref[...], 3), 16)

    @task(5.5)
    def _():
        v = lax.dot_general(svs, wd[...], NT, preferred_element_type=F32)
        vv[...] = stacked(split(v[0:1] + v[1:2] + v[2:3], 3), 16)

    @task(9.0)
    def _():
        got["o1"].wait_recv()
        got["o2"] = send([(ow.at[:, 0, 0], ow.at[:, 0, j], dev(dy=-side[j])) for j in (1, 2, 3)],
                         ow.at[:, 0, pl.ds(1, 3)])

    @task(13.0)
    def _():
        got["o2"].wait_recv()
        got["o3"] = send([(ow.at[:, 0], ow.at[:, n], dev(dz=-near[n])) for n in (1, 2, 3)], ow.at[:, pl.ds(1, 3)])

    lane_h = lax.broadcasted_iota(jnp.int32, (half, 128), 1)

    def pair_tile(sq):
        hi, lo = split(sq, 2)
        return jnp.where(lane_h == 0, hi.astype(F32), jnp.where(lane_h == 1, lo.astype(F32), 0.0))

    def product(w, core):
        part = x[w, pl.ds(2 * core, 2)].reshape(half, feats)
        wide = part.astype(F32)
        sq = jnp.sum(wide * wide, axis=1, keepdims=True)
        return jnp.dot(part, wt[...], preferred_element_type=F32), pair_tile(sq)

    for w in range(NW):
        at = ready[w]

        @task(at)
        def _(w=w):
            got["p3", w].wait_recv()
            got["q3", w].wait_recv()
            gu, sq = product(w, 1 - cc)
            gus[w, :, pl.ds(0, width)] = gu.astype(BF)
            gus[w, :, pl.ds(width, 128)] = sq.astype(BF)
            got["c1", w] = send([(gus.at[w], rc.at[w], dev(other=True))], rc.at[w])
            gu, sq = product(w, cc)
            guo[w, :, :, pl.ds(0, width)] = gu.reshape(NX, blk, width)
            guo[w, :, :, pl.ds(width, 128)] = sq.reshape(NX, blk, 128)

        @task(at + 1.6)
        def _(w=w):
            got["c1", w].wait_recv()
            total = guo[w].reshape(half, width + 128) + rc[w].astype(F32)
            sq = pair_tile(total[:, width:width + 1] + total[:, width + 1:width + 2])
            guo[w, :, :, pl.ds(0, width)] = total[:, 0:width].reshape(NX, blk, width)
            guo[w, :, :, pl.ds(width, 128)] = sq.reshape(NX, blk, 128)
            gub[w, :, :, pl.ds(0, width)] = total[:, 0:width].astype(BF).reshape(NX, blk, width)
            gub[w, :, :, pl.ds(width, 128)] = sq.astype(BF).reshape(NX, blk, 128)
            got["x", w] = send([(gub.at[w, (xx + dx) % NX], rx.at[w, dx - 1], dev(dx=dx)) for dx in (2, 1, 3)], rx.at[w])

        @task(at + 5.6)
        def _(w=w):
            got["x", w].wait_recv()
            gu = guo[w, xx]
            for i in range(NX - 1):
                gu = gu + rx[w, i].astype(F32)
            sq = gu[:, width:width + 1] + gu[:, width + 1:width + 2]
            gu = gu[:, 0:width] * lax.rsqrt(sq / (feats * NX * 2) + EPS)

            def act(gate, up):
                return (gate / (1.0 + jnp.exp(-gate)) * up).astype(BF)

            if full:
                hid[w, cc, xx, :, pl.ds(0, full)] = act(gu[:, 0:full], gu[:, full:2 * full])
            if rest:
                last = gu[:, 2 * full:]
                at_lane = lax.broadcasted_iota(jnp.int32, last.shape, 1)
                value = act(last, pltpu.roll(last, 128 - rest, 1))
                hid[w, cc, xx, :, pl.ds(full, 128)] = jnp.where(at_lane < rest, value, jnp.zeros_like(value))
            done = hid.at[w, cc, xx]
            got["h", w] = send([(done, done, dev(dx=dx)) for dx in (2, 1, 3)], hid.at[w, cc, pl.ds(0, NX - 1)])

        @task(at + 9.4)
        def _(w=w):
            got["h", w].wait_recv()
            got["c2", w] = send([(hid.at[w, cc], hid.at[w, cc], dev(other=True))], hid.at[w, cc])

        @task(at + 10.4)
        def _(w=w):
            got["c2", w].wait_recv()
            act = hid[w].reshape(2 * half, hpad)
            down = jnp.dot(act, wd[...], preferred_element_type=F32)
            pt[w] = down.astype(BF).reshape(4, NY, rows, feats)
            got["r1p", w] = send([(pt.at[w, n, :, :, A], r1p.at[w, n - 1], dev(dz=near[n])) for n in (1, 2, 3)], r1p.at[w])
            got["r1q", w] = send([(pt.at[w, :, j, :, B], r1q.at[w, j - 1], dev(dy=side[j])) for j in (1, 2, 3)], r1q.at[w])
            v = lax.dot_general(vv[...], act, NT, preferred_element_type=F32)
            rsc[w] = v[0:8]

        @task(at + 15.0)
        def _(w=w):
            got["r1p", w].wait_recv()
            v = pt[w, 0, :, :, A].astype(F32)
            for i in range(3):
                v = v + r1p[w, i].astype(F32)
            pt[w, 0, :, :, A] = v.astype(BF)
            got["r2p", w] = send([(pt.at[w, 0, j, :, A], r2p.at[w, j - 1], dev(dy=side[j])) for j in (1, 2, 3)], r2p.at[w])

        @task(at + 15.1)
        def _(w=w):
            got["r1q", w].wait_recv()
            v = pt[w, :, 0, :, B].astype(F32)
            for i in range(3):
                v = v + r1q[w, i].astype(F32)
            pt[w, :, 0, :, B] = v.astype(BF)
            got["r2q", w] = send([(pt.at[w, n, 0, :, B], r2q.at[w, n - 1], dev(dz=near[n])) for n in (1, 2, 3)], r2q.at[w])

        @task(at + 18.8)
        def _(w=w):
            got["r2p", w].wait_recv()
            got["r2q", w].wait_recv()
            a, b = pt[w, 0, 0, :, A].astype(F32), pt[w, 0, 0, :, B].astype(F32)
            for i in range(3):
                a, b = a + r2p[w, i].astype(F32), b + r2q[w, i].astype(F32)
            fs[w, :, A] = a.astype(BF)
            fs[w, :, B] = b.astype(BF)
            if w:
                got["rf", w] = send([(fs.at[w], rf.at[w - 1], dev(dz=FAR[w]))], rf.at[w - 1])

    bases = (0, len(tp_peers) + 1, len(tp_peers) + len(y_peers) + 2)

    def exchange(key, base, value, peers):
        sc[base] = value
        got[key] = send([(sc.at[base], sc.at[base + 1 + i], peer) for i, peer in enumerate(peers)],
                        sc.at[pl.ds(base + 1, len(peers))])

    def collect(key, base, peers):
        got[key].wait_recv()
        v = sc[base]
        for i in range(len(peers)):
            v = v + sc[base + 1 + i]
        return v

    keep = {}
    last_d = ready[NW - 1] + 10.4

    @task(last_d + 0.1)
    def _():
        got["o3"].wait_recv()
        direct = lax.dot_general(svs, x[0, pl.ds(0, 2)].reshape(half, feats), NT, preferred_element_type=F32)
        direct = jnp.where(lane < rows, direct[0:1] + direct[1:2] + direct[2:3], 0.0)
        cand = lax.broadcasted_iota(jnp.int32, (128, 128), 0)
        per = 128 // rows
        sums = jnp.zeros((16, 128), F32)
        for w in range(NW):
            for h in range(2):
                who = jnp.zeros((1, 128), jnp.int32)
                for p in range(per):
                    who = jnp.where(lane // rows == p, ow[w, 2 * h + p // NY, p % NY], who)
                score = rsc[w, :, pl.ds(h * 128, 128)]
                score = score[0:1] + score[1:2] + score[2:3]
                if w == 0 and h == 0:
                    score = score + direct
                terms = stacked(split(score, 3) + [jnp.ones((1, 128), BF)], 16)
                sums = sums + lax.dot_general(terms, jnp.where(cand == who, 1.0, 0.0).astype(BF), NT,
                                              preferred_element_type=F32)
        keep["count"] = sums[3:4]
        exchange("s1", bases[0], sums[0:1] + sums[1:2] + sums[2:3], tp_peers)

    @task(last_d + 4.5)
    def _():
        exchange("s2", bases[1], collect("s1", bases[0], tp_peers), y_peers)

    @task(last_d + 8.3)
    def _():
        exchange("s3", bases[2], collect("s2", bases[1], y_peers), z_peers)

    for _, _, fn in sorted(tasks, key=lambda item: item[:2]):
        fn()

    v = fs[0].astype(F32)
    for w in range(1, NW):
        got["rf", w].wait_recv()
        v = v + rf[w - 1].astype(F32)
    out_ref[...] = (v + prev_ref[...].astype(F32)).astype(BF)
    assert used[0] == ssem.shape[0]
    score_ref[...] = collect("s3", bases[2], z_peers) / keep["count"]
    for copy in flying:
        copy.wait_send()


def shards(preview, row_owner, norm_gain, w_gate, w_up, w_down, score_vec):
    rows, feats = preview.shape
    hidden = w_gate.shape[0]
    hpad = -(-hidden // 128) * 128
    half, blk, wide = 2 * NY * rows, 2 * NY * rows // NX, 2 * hidden + 128
    pa = max(1, feats // 128 * 3 // 8) * 128
    pb = feats - pa
    sems = 60
    vmem = pl.BlockSpec(memory_space=pltpu.VMEM)
    hbm = pl.BlockSpec(memory_space=pl.ANY)
    verified, scores = pl.pallas_call(
        functools.partial(kernel, pa),
        out_shape=(jax.ShapeDtypeStruct((rows, feats), BF), jax.ShapeDtypeStruct((1, 128), F32)),
        in_specs=[vmem, pl.BlockSpec(memory_space=pltpu.SMEM), vmem, hbm, hbm, hbm, vmem],
        out_specs=(vmem, vmem),
        scratch_shapes=[
            pltpu.VMEM((NW, 4, NY, rows, feats), BF),
            pltpu.VMEM((2 * hidden, feats), BF),
            pltpu.VMEM((feats, 2 * hidden), BF),
            pltpu.VMEM((hpad, feats), BF),
            pltpu.VMEM((16, hpad), BF),
            pltpu.VMEM((NW, half, wide), BF),
            pltpu.VMEM((NW, NX, blk, wide), F32),
            pltpu.VMEM((NW, NX, blk, wide), BF),
            pltpu.VMEM((NW, half, wide), BF),
            pltpu.VMEM((NW, NX - 1, blk, wide), BF),
            pltpu.VMEM((NW, 2, NX, blk, hpad), BF),
            pltpu.VMEM((NW, 4, NY, rows, feats), BF),
            pltpu.VMEM((NW, 3, NY, rows, pa), BF),
            pltpu.VMEM((NW, 3, 4, rows, pb), BF),
            pltpu.VMEM((NW, 3, rows, pa), BF),
            pltpu.VMEM((NW, 3, rows, pb), BF),
            pltpu.VMEM((NW, rows, feats), BF),
            pltpu.VMEM((NW - 1, rows, feats), BF),
            pltpu.VMEM((NW, 4, NY, 1, 128), jnp.int32),
            pltpu.VMEM((NW, 8, 2 * half), F32),
            pltpu.VMEM((2 * NX + NY + NZ, 1, 128), F32),
            pltpu.SemaphoreType.DMA((5,)),
            pltpu.SemaphoreType.DMA((sems,)),
            pltpu.SemaphoreType.DMA((sems,)),
        ],
        compiler_params=pltpu.CompilerParams(
            collective_id=0, has_side_effects=True, vmem_limit_bytes=56 << 20),
    )(preview, row_owner, norm_gain[None, :], w_gate, w_up, w_down, score_vec[None, :])
    return verified, scores[0, :CAND]


def solution(mesh):
    placed = (
        P("section", "tp"),
        P("section"),
        P("tp"),
        P("section", "tp"),
        P("section", "tp"),
        P("section", "tp"),
        P("tp"),
    )
    return jax.shard_map(
        shards, mesh=mesh, in_specs=placed, out_specs=(P("section", "tp"), P()), check_vma=False
    )
```

time: 654 us -> 89 us (0.14)
  the two profiles are of different devices: /device:TPU:1 before, /device:TPU:8 now
where the time goes in v2:
time: 89 us; the launch traced here: 88.8 us
  Pallas kernels  85.6 us (96%)
  local copies, waits for them, and re-layouts  2.51 us (3%)
    pallas_call x1, Pallas kernels, shards(): pl.pallas_call(functools.partial(kernel, pa), out_shape=(jax.ShapeDtypeSt...  85.6 us
    unnamed x3, local copies, waits for them, and re-layouts  2 us

profile of v2, /device:TPU:8, one launch (start us, length us, event | category | flops | bytes accessed | tf_op | source)
XLA Modules:
  0.0 88.8 jit_solution(117456746579842413)
XLA Ops:
  0.6 85.6 %shard_map.86 = (bf16[16,1024]{1,0:T(8,128)(2,1)}, f32[1,128]{1,0:T(1,128)}) custom-call(bf16[16,1024]{1,0:T(8,128)(2,1)} %prev_ref.1, s32[16]{0:T(128)} %owner_ref.1, f32[1,1024]{1,0:T(1,128)} %bitcast.4, bf16[448,1024]{1,0:T(8,128)(2,1)} %wg_ref.1, bf16[448,1024]{1,0:T(8,128)(2,1)} %wu_ref.1, bf16[448,1024]{1,0:T(8,128)(2,1)} %wd_ref.1, f32[1,1024]{1,0:T(1,128)} %bitcast.5), custom_call_target="tpu_custom_call" | custom-call | tf_op jit(solution)/shard_map/pallas_call | solution.py:352
  86.3 0.0 copy-start
  86.3 0.6 copy-done
  86.9 0.5 slice_bitcast_fusion
  87.4 1.4 %copy.10 = bf16[16,1024]{1,0:T(8,128)(2,1)} copy(bf16[16,1024]{1,0:T(8,128)(2,1)} %get-tuple-element.8) | data formatting | bytes 65536
Async XLA Ops:
  86.3 0.6 copy-start

commit v3 on v2

--- a/solution.py
+++ b/solution.py
@@ -16,6 +16,13 @@
 FAR = (0, 4, -4, 8)
 NT = (((1,), (1,)), ((), ()))
 MESH = pl.DeviceIdType.MESH
+ORDER = (
+    "far2", "far3", "nq", "wts", "s0", "far1", "nrm", "s2", "p0", "q0", "s1", "s3",
+    "q2", "p2", "vec", "m0", "own2", "q3", "p3", "x0", "own3", "p1", "m2", "q1",
+    "x2", "m3", "h0", "x3", "m1", "h2", "x1", "h3", "c0", "c2", "d0", "d2",
+    "h1", "c3", "d3", "c1", "d1", "v1", "f3", "e3", "e0", "f0", "f2", "e2",
+    "v2", "f1", "e1", "g3", "g0", "v3", "g1", "g2",
+)
 
 
 def split(v, parts):
@@ -36,10 +43,10 @@
     return out.astype(BF)
 
 
-def kernel(pa, prev_ref, owner_ref, gain_ref, wg_ref, wu_ref, wd_ref, sv_ref, out_ref, score_ref,
-           x, wgu, wt, wd, vv, gus, guo, gub, rc, rx, hid, pt, r1p, r1q, r2p, r2q, fs, rf, ow, rsc, sc,
+def kernel(pa, prev_hbm, owner_ref, gain_hbm, wg_ref, wu_ref, wd_ref, sv_hbm, out_ref, score_ref,
+           prev_ref, gain_ref, sv_ref, x, wgu, wt, wd, vv, sv3, nq, gus, guo, gub, rc, rx, hid, pt, r1p, r1q, r2p, r2q, fs, rf, ow, rsc, sc,
            lsem, ssem, rsem):
-    rows, feats, hidden = prev_ref.shape[0], prev_ref.shape[1], wg_ref.shape[0]
+    rows, feats, hidden = prev_hbm.shape[0], prev_hbm.shape[1], wg_ref.shape[0]
     hpad = -(-hidden // 128) * 128
     full = hidden // 128 * 128
     rest = hidden - full
@@ -70,6 +77,12 @@
         flying.append(whole)
         return whole
 
+    tp_peers = [dev(dx=dx, other=o) for dx in range(NX) for o in (False, True) if (dx, o) != (0, False)]
+    y_peers = [dev(dy=dy) for dy in range(1, NY)]
+    z_peers = [dev(dz=dz) for dz in range(1, NZ)]
+    barrier = pltpu.get_barrier_semaphore()
+    for peer in z_peers + y_peers + tp_peers:
+        pl.semaphore_signal(barrier, inc=1, device_id=peer, device_id_type=MESH)
     loads = []
 
     def load(src, dst):
@@ -77,6 +90,9 @@
         copy.start()
         loads.append(copy)
 
+    load(prev_hbm, prev_ref)
+    load(gain_hbm, gain_ref)
+    load(sv_hbm, sv_ref)
     if full:
         load(wg_ref.at[pl.ds(0, full)], wgu.at[pl.ds(0, full)])
         load(wu_ref.at[pl.ds(0, full)], wgu.at[pl.ds(full, full)])
@@ -86,27 +102,25 @@
     load(wd_ref, wd.at[pl.ds(0, hidden)])
     if rest:
         wd[pl.ds(hidden, hpad - hidden), :] = jnp.zeros((hpad - hidden, feats), BF)
+    loads[0].wait()
     x[0, 0, 0] = prev_ref[...]
     lane = lax.broadcasted_iota(jnp.int32, (1, 128), 1)
-    mine = jnp.zeros((1, 128), jnp.int32)
+    owner = jnp.zeros((1, 128), F32)
     for r in range(rows):
-        mine = jnp.where(lane % rows == r, owner_ref[r], mine)
-    ow[0, 0, 0] = mine
-
-    tp_peers = [dev(dx=dx, other=o) for dx in range(NX) for o in (False, True) if (dx, o) != (0, False)]
-    y_peers = [dev(dy=dy) for dy in range(1, NY)]
-    z_peers = [dev(dz=dz) for dz in range(1, NZ)]
-    barrier = pltpu.get_barrier_semaphore()
-    for peer in z_peers + y_peers + tp_peers:
-        pl.semaphore_signal(barrier, inc=1, device_id=peer, device_id_type=MESH)
+        owner = jnp.where(lane % rows == r, owner_ref[r].astype(F32), owner)
+    own = prev_ref[...].astype(F32)
+    sq = jnp.sum(own * own, axis=1, keepdims=True)
+    eye = (lax.broadcasted_iota(jnp.int32, (rows, 128), 1) % rows
+           == lax.broadcasted_iota(jnp.int32, (rows, 128), 0))
+    nq[0] = jnp.sum(jnp.where(eye, sq, 0.0), axis=0, keepdims=True)
     pl.semaphore_wait(barrier, len(tp_peers + y_peers + z_peers))
 
     got = {}
-    tasks = []
-
-    def task(when):
+    tasks = {}
+
+    def task(name):
         def add(fn):
-            tasks.append((when, len(tasks), fn))
+            tasks[name] = fn
             return fn
         return add
 
@@ -116,107 +130,112 @@
         got["q2", w] = send([(x.at[w, 0, 0, :, B], x.at[w, n, 0, :, B], dev(dz=-near[n])) for n in (1, 2, 3)],
                             x.at[w, pl.ds(1, 3), 0, :, B])
 
-    for w in (3, 1, 2):
-        got["far", w] = send([(x.at[0, 0, 0], x.at[w, 0, 0], dev(dz=-FAR[w]))], x.at[w, 0, 0])
-    spread(0)
-    got["o1"] = send([(ow.at[0, 0, 0], ow.at[w, 0, 0], dev(dz=-FAR[w])) for w in (1, 2, 3)], ow.at[pl.ds(1, 3), 0, 0])
-
-    begin = {0: 0.0, 1: 4.8, 2: 4.9, 3: 7.4}
-    ready = {0: 8.0, 1: 12.0, 2: 14.0, 3: 16.5}
-
     for w in range(NW):
         if w:
-            @task(begin[w])
+            @task(f"far{w}")
             def _(w=w):
+                got["far", w] = send([(x.at[0, 0, 0], x.at[w, 0, 0], dev(dz=-FAR[w]))], x.at[w, 0, 0])
+
+        @task(f"s{w}")
+        def _(w=w):
+            if w:
                 got["far", w].wait_recv()
-                spread(w)
-
-        @task(begin[w] + 3.2)
+            spread(w)
+
+        @task(f"p{w}")
         def _(w=w):
             got["p2", w].wait_recv()
             got["p3", w] = send([(x.at[w, 0, :, :, A], x.at[w, n, :, :, A], dev(dz=-near[n])) for n in (1, 2, 3)],
                                 x.at[w, pl.ds(1, 3), :, :, A])
 
-        @task(begin[w] + 3.3)
+        @task(f"q{w}")
         def _(w=w):
             got["q2", w].wait_recv()
             got["q3", w] = send([(x.at[w, :, 0, :, B], x.at[w, :, j, :, B], dev(dy=-side[j])) for j in (1, 2, 3)],
                                 x.at[w, :, pl.ds(1, 3), :, B])
 
-    step = 128
-    for i in range(width // step):
-        @task(0.1 + 0.3 * i)
-        def _(i=i):
-            if i == 0:
-                for copy in loads:
-                    copy.wait()
-            piece = wgu[pl.ds(i * step, step), :].astype(F32) * gain_ref[...]
-            wt[:, pl.ds(i * step, step)] = piece.astype(BF).T
-
-    svs = stacked(split(sv_ref[...], 3), 16)
-
-    @task(5.5)
-    def _():
-        v = lax.dot_general(svs, wd[...], NT, preferred_element_type=F32)
-        vv[...] = stacked(split(v[0:1] + v[1:2] + v[2:3], 3), 16)
-
-    @task(9.0)
+    @task("nq")
+    def _():
+        got["nq"] = send([(nq.at[0], nq.at[i + 1], peer) for i, peer in enumerate(tp_peers)],
+                         nq.at[pl.ds(1, len(tp_peers))])
+
+    @task("nrm")
+    def _():
+        got["nq"].wait_recv()
+        total = nq[0]
+        for i in range(len(tp_peers)):
+            total = total + nq[i + 1]
+        ow[0, 0, 0, 0:1] = owner
+        ow[0, 0, 0, 1:2] = lax.rsqrt(total / (feats * NX * 2) + EPS)
+        got["o1"] = send([(ow.at[0, 0, 0], ow.at[w, 0, 0], dev(dz=-FAR[w])) for w in (1, 2, 3)],
+                         ow.at[pl.ds(1, 3), 0, 0])
+
+    @task("own2")
     def _():
         got["o1"].wait_recv()
         got["o2"] = send([(ow.at[:, 0, 0], ow.at[:, 0, j], dev(dy=-side[j])) for j in (1, 2, 3)],
                          ow.at[:, 0, pl.ds(1, 3)])
 
-    @task(13.0)
+    @task("own3")
     def _():
         got["o2"].wait_recv()
         got["o3"] = send([(ow.at[:, 0], ow.at[:, n], dev(dz=-near[n])) for n in (1, 2, 3)], ow.at[:, pl.ds(1, 3)])
 
-    lane_h = lax.broadcasted_iota(jnp.int32, (half, 128), 1)
-
-    def pair_tile(sq):
-        hi, lo = split(sq, 2)
-        return jnp.where(lane_h == 0, hi.astype(F32), jnp.where(lane_h == 1, lo.astype(F32), 0.0))
+    have = []
+
+    def owners():
+        if not have:
+            got["o3"].wait_recv()
+            have.append(True)
+
+    step = 128
+
+    @task("wts")
+    def _():
+        for copy in loads[1:]:
+            copy.wait()
+        for i in range(width // step):
+            piece = wgu[pl.ds(i * step, step), :].astype(F32) * gain_ref[...]
+            wt[:, pl.ds(i * step, step)] = piece.astype(BF).T
+
+    @task("vec")
+    def _():
+        sv3[...] = stacked(split(sv_ref[...], 3), 16)
+        v = lax.dot_general(sv3[...], wd[...], NT, preferred_element_type=F32)
+        vv[...] = stacked(split(v[0:1] + v[1:2] + v[2:3], 3), 16)
 
     def product(w, core):
         part = x[w, pl.ds(2 * core, 2)].reshape(half, feats)
-        wide = part.astype(F32)
-        sq = jnp.sum(wide * wide, axis=1, keepdims=True)
-        return jnp.dot(part, wt[...], preferred_element_type=F32), pair_tile(sq)
+        return jnp.dot(part, wt[...], preferred_element_type=F32)
 
     for w in range(NW):
-        at = ready[w]
-
-        @task(at)
+        @task(f"m{w}")
         def _(w=w):
             got["p3", w].wait_recv()
             got["q3", w].wait_recv()
-            gu, sq = product(w, 1 - cc)
-            gus[w, :, pl.ds(0, width)] = gu.astype(BF)
-            gus[w, :, pl.ds(width, 128)] = sq.astype(BF)
+            gus[w] = product(w, 1 - cc).astype(BF)
             got["c1", w] = send([(gus.at[w], rc.at[w], dev(other=True))], rc.at[w])
-            gu, sq = product(w, cc)
-            guo[w, :, :, pl.ds(0, width)] = gu.reshape(NX, blk, width)
-            guo[w, :, :, pl.ds(width, 128)] = sq.reshape(NX, blk, 128)
-
-        @task(at + 1.6)
+            guo[w] = product(w, cc).reshape(NX, blk, width)
+
+        @task(f"x{w}")
         def _(w=w):
             got["c1", w].wait_recv()
-            total = guo[w].reshape(half, width + 128) + rc[w].astype(F32)
-            sq = pair_tile(total[:, width:width + 1] + total[:, width + 1:width + 2])
-            guo[w, :, :, pl.ds(0, width)] = total[:, 0:width].reshape(NX, blk, width)
-            guo[w, :, :, pl.ds(width, 128)] = sq.reshape(NX, blk, 128)
-            gub[w, :, :, pl.ds(0, width)] = total[:, 0:width].astype(BF).reshape(NX, blk, width)
-            gub[w, :, :, pl.ds(width, 128)] = sq.astype(BF).reshape(NX, blk, 128)
+            total = guo[w] + rc[w].astype(F32).reshape(NX, blk, width)
+            guo[w] = total
+            gub[w] = total.astype(BF)
             got["x", w] = send([(gub.at[w, (xx + dx) % NX], rx.at[w, dx - 1], dev(dx=dx)) for dx in (2, 1, 3)], rx.at[w])
 
-        @task(at + 5.6)
-        def _(w=w):
+        @task(f"h{w}")
+        def _(w=w):
+            owners()
             got["x", w].wait_recv()
             gu = guo[w, xx]
             for i in range(NX - 1):
                 gu = gu + rx[w, i].astype(F32)
-            sq = gu[:, width:width + 1] + gu[:, width + 1:width + 2]
-            gu = gu[:, 0:width] * lax.rsqrt(sq / (feats * NX * 2) + EPS)
+            scales = [ow[w, 2 * cc + xx // 2, 2 * (xx % 2) + i][1:2] for i in range(2)]
+            scale = jnp.concatenate([jnp.sum(jnp.where(eye & (lane < rows), sc_, 0.0), axis=1, keepdims=True)
+                                     for sc_ in scales], axis=0)
+            gu = gu * scale
 
             def act(gate, up):
                 return (gate / (1.0 + jnp.exp(-gate)) * up).astype(BF)
@@ -231,12 +250,12 @@
             done = hid.at[w, cc, xx]
             got["h", w] = send([(done, done, dev(dx=dx)) for dx in (2, 1, 3)], hid.at[w, cc, pl.ds(0, NX - 1)])
 
-        @task(at + 9.4)
+        @task(f"c{w}")
         def _(w=w):
             got["h", w].wait_recv()
             got["c2", w] = send([(hid.at[w, cc], hid.at[w, cc], dev(other=True))], hid.at[w, cc])
 
-        @task(at + 10.4)
+        @task(f"d{w}")
         def _(w=w):
             got["c2", w].wait_recv()
             act = hid[w].reshape(2 * half, hpad)
@@ -247,7 +266,7 @@
             v = lax.dot_general(vv[...], act, NT, preferred_element_type=F32)
             rsc[w] = v[0:8]
 
-        @task(at + 15.0)
+        @task(f"e{w}")
         def _(w=w):
             got["r1p", w].wait_recv()
             v = pt[w, 0, :, :, A].astype(F32)
@@ -256,7 +275,7 @@
             pt[w, 0, :, :, A] = v.astype(BF)
             got["r2p", w] = send([(pt.at[w, 0, j, :, A], r2p.at[w, j - 1], dev(dy=side[j])) for j in (1, 2, 3)], r2p.at[w])
 
-        @task(at + 15.1)
+        @task(f"f{w}")
         def _(w=w):
             got["r1q", w].wait_recv()
             v = pt[w, :, 0, :, B].astype(F32)
@@ -265,7 +284,7 @@
             pt[w, :, 0, :, B] = v.astype(BF)
             got["r2q", w] = send([(pt.at[w, n, 0, :, B], r2q.at[w, n - 1], dev(dz=near[n])) for n in (1, 2, 3)], r2q.at[w])
 
-        @task(at + 18.8)
+        @task(f"g{w}")
         def _(w=w):
             got["r2p", w].wait_recv()
             got["r2q", w].wait_recv()
@@ -292,21 +311,19 @@
         return v
 
     keep = {}
-    last_d = ready[NW - 1] + 10.4
-
-    @task(last_d + 0.1)
-    def _():
-        got["o3"].wait_recv()
-        direct = lax.dot_general(svs, x[0, pl.ds(0, 2)].reshape(half, feats), NT, preferred_element_type=F32)
+    @task("v1")
+    def _():
+        owners()
+        direct = lax.dot_general(sv3[...], x[0, pl.ds(0, 2)].reshape(half, feats), NT, preferred_element_type=F32)
         direct = jnp.where(lane < rows, direct[0:1] + direct[1:2] + direct[2:3], 0.0)
-        cand = lax.broadcasted_iota(jnp.int32, (128, 128), 0)
+        cand = lax.broadcasted_iota(jnp.int32, (128, 128), 0).astype(F32)
         per = 128 // rows
         sums = jnp.zeros((16, 128), F32)
         for w in range(NW):
             for h in range(2):
-                who = jnp.zeros((1, 128), jnp.int32)
+                who = jnp.zeros((1, 128), F32)
                 for p in range(per):
-                    who = jnp.where(lane // rows == p, ow[w, 2 * h + p // NY, p % NY], who)
+                    who = jnp.where(lane // rows == p, ow[w, 2 * h + p // NY, p % NY][0:1], who)
                 score = rsc[w, :, pl.ds(h * 128, 128)]
                 score = score[0:1] + score[1:2] + score[2:3]
                 if w == 0 and h == 0:
@@ -317,16 +334,17 @@
         keep["count"] = sums[3:4]
         exchange("s1", bases[0], sums[0:1] + sums[1:2] + sums[2:3], tp_peers)
 
-    @task(last_d + 4.5)
+    @task("v2")
     def _():
         exchange("s2", bases[1], collect("s1", bases[0], tp_peers), y_peers)
 
-    @task(last_d + 8.3)
+    @task("v3")
     def _():
         exchange("s3", bases[2], collect("s2", bases[1], y_peers), z_peers)
 
-    for _, _, fn in sorted(tasks, key=lambda item: item[:2]):
-        fn()
+    assert sorted(ORDER) == sorted(tasks)
+    for name in ORDER:
+        tasks[name]()
 
     v = fs[0].astype(F32)
     for w in range(1, NW):
@@ -343,23 +361,28 @@
     rows, feats = preview.shape
     hidden = w_gate.shape[0]
     hpad = -(-hidden // 128) * 128
-    half, blk, wide = 2 * NY * rows, 2 * NY * rows // NX, 2 * hidden + 128
-    pa = max(1, feats // 128 * 3 // 8) * 128
+    half, blk, wide = 2 * NY * rows, 2 * NY * rows // NX, 2 * hidden
+    pa = feats // 256 * 128
     pb = feats - pa
-    sems = 60
+    sems = 61
     vmem = pl.BlockSpec(memory_space=pltpu.VMEM)
     hbm = pl.BlockSpec(memory_space=pl.ANY)
     verified, scores = pl.pallas_call(
         functools.partial(kernel, pa),
         out_shape=(jax.ShapeDtypeStruct((rows, feats), BF), jax.ShapeDtypeStruct((1, 128), F32)),
-        in_specs=[vmem, pl.BlockSpec(memory_space=pltpu.SMEM), vmem, hbm, hbm, hbm, vmem],
+        in_specs=[hbm, pl.BlockSpec(memory_space=pltpu.SMEM), hbm, hbm, hbm, hbm, hbm],
         out_specs=(vmem, vmem),
         scratch_shapes=[
+            pltpu.VMEM((rows, feats), BF),
+            pltpu.VMEM((1, feats), F32),
+            pltpu.VMEM((1, feats), F32),
             pltpu.VMEM((NW, 4, NY, rows, feats), BF),
             pltpu.VMEM((2 * hidden, feats), BF),
             pltpu.VMEM((feats, 2 * hidden), BF),
             pltpu.VMEM((hpad, feats), BF),
             pltpu.VMEM((16, hpad), BF),
+            pltpu.VMEM((16, feats), BF),
+            pltpu.VMEM((2 * NX, 1, 128), F32),
             pltpu.VMEM((NW, half, wide), BF),
             pltpu.VMEM((NW, NX, blk, wide), F32),
             pltpu.VMEM((NW, NX, blk, wide), BF),
@@ -373,10 +396,10 @@
             pltpu.VMEM((NW, 3, rows, pb), BF),
             pltpu.VMEM((NW, rows, feats), BF),
             pltpu.VMEM((NW - 1, rows, feats), BF),
-            pltpu.VMEM((NW, 4, NY, 1, 128), jnp.int32),
+            pltpu.VMEM((NW, 4, NY, 2, 128), F32),
             pltpu.VMEM((NW, 8, 2 * half), F32),
             pltpu.VMEM((2 * NX + NY + NZ, 1, 128), F32),
-            pltpu.SemaphoreType.DMA((5,)),
+            pltpu.SemaphoreType.DMA((8,)),
             pltpu.SemaphoreType.DMA((sems,)),
             pltpu.SemaphoreType.DMA((sems,)),
         ],

time: 89 us -> 79.8 us (0.90)
  the two profiles are of different devices: /device:TPU:8 before, /device:TPU:1 now
where the time goes in v3:
time: 79.8 us; the launch traced here: 78.8 us
  Pallas kernels  75.6 us (95%)
  local copies, waits for them, and re-layouts  2.51 us (3%)
    pallas_call x1, Pallas kernels, shards(): pl.pallas_call(functools.partial(kernel, pa), out_shape=(jax.ShapeDtypeSt...  75.6 us
    unnamed x3, local copies, waits for them, and re-layouts  2 us

profile of v3, /device:TPU:1, one launch (start us, length us, event | category | flops | bytes accessed | tf_op | source)
XLA Modules:
  0.0 78.8 jit_solution(7110406252583066954)
XLA Ops:
  0.6 75.6 %shard_map.86 = (bf16[16,1024]{1,0:T(8,128)(2,1)}, f32[1,128]{1,0:T(1,128)}) custom-call(bf16[16,1024]{1,0:T(8,128)(2,1)} %prev_hbm.1, s32[16]{0:T(128)} %owner_ref.1, f32[1,1024]{1,0:T(1,128)} %bitcast.4, bf16[448,1024]{1,0:T(8,128)(2,1)} %wg_ref.1, bf16[448,1024]{1,0:T(8,128)(2,1)} %wu_ref.1, bf16[448,1024]{1,0:T(8,128)(2,1)} %wd_ref.1, f32[1,1024]{1,0:T(1,128)} %bitcast.5), custom_call_target="tpu_custom_call" | custom-call | tf_op jit(solution)/shard_map/pallas_call | solution.py:370
  76.3 0.0 copy-start
  76.3 0.6 copy-done
  76.9 0.5 slice_bitcast_fusion
  77.4 1.4 %copy.10 = bf16[16,1024]{1,0:T(8,128)(2,1)} copy(bf16[16,1024]{1,0:T(8,128)(2,1)} %get-tuple-element.8) | data formatting | bytes 65536
Async XLA Ops:
  76.3 0.6 copy-start

commit v4 on v3

--- a/solution.py
+++ b/solution.py
@@ -17,11 +17,11 @@
 NT = (((1,), (1,)), ((), ()))
 MESH = pl.DeviceIdType.MESH
 ORDER = (
-    "far2", "far3", "nq", "wts", "s0", "far1", "nrm", "s2", "p0", "q0", "s1", "s3",
-    "q2", "p2", "vec", "m0", "own2", "q3", "p3", "x0", "own3", "p1", "m2", "q1",
-    "x2", "m3", "h0", "x3", "m1", "h2", "x1", "h3", "c0", "c2", "d0", "d2",
-    "h1", "c3", "d3", "c1", "d1", "v1", "f3", "e3", "e0", "f0", "f2", "e2",
-    "v2", "f1", "e1", "g3", "g0", "v3", "g1", "g2",
+    "far2", "nq", "wts", "far3", "s0", "far1", "nrm", "s2", "p0", "q0", "s1", "s3",
+    "q2", "vec", "p2", "own2", "m0", "q3", "q1", "p3", "x0", "m2", "own3", "p1",
+    "x2", "m3", "h0", "x3", "m1", "h2", "c0", "x1", "h3", "d0", "c2", "d2",
+    "h1", "c3", "d3", "c1", "f2", "d1", "v1", "f3", "e3", "f0", "e2", "v2",
+    "f1", "g3", "e1", "e0", "v3", "g2", "g1", "g0",
 )
 
 
@@ -350,7 +350,7 @@
     for w in range(1, NW):
         got["rf", w].wait_recv()
         v = v + rf[w - 1].astype(F32)
-    out_ref[...] = (v + prev_ref[...].astype(F32)).astype(BF)
+    out_ref[...] = v
     assert used[0] == ssem.shape[0]
     score_ref[...] = collect("s3", bases[2], z_peers) / keep["count"]
     for copy in flying:
@@ -369,7 +369,7 @@
     hbm = pl.BlockSpec(memory_space=pl.ANY)
     verified, scores = pl.pallas_call(
         functools.partial(kernel, pa),
-        out_shape=(jax.ShapeDtypeStruct((rows, feats), BF), jax.ShapeDtypeStruct((1, 128), F32)),
+        out_shape=(jax.ShapeDtypeStruct((rows, feats), F32), jax.ShapeDtypeStruct((1, 128), F32)),
         in_specs=[hbm, pl.BlockSpec(memory_space=pltpu.SMEM), hbm, hbm, hbm, hbm, hbm],
         out_specs=(vmem, vmem),
         scratch_shapes=[
@@ -406,7 +406,7 @@
         compiler_params=pltpu.CompilerParams(
             collective_id=0, has_side_effects=True, vmem_limit_bytes=56 << 20),
     )(preview, row_owner, norm_gain[None, :], w_gate, w_up, w_down, score_vec[None, :])
-    return verified, scores[0, :CAND]
+    return (verified + preview.astype(F32)).astype(BF), scores[0, :CAND]
 
 
 def solution(mesh):

time: 79.8 us -> 78.1 us (0.979)
  the two profiles are of different devices: /device:TPU:1 before, /device:TPU:32 now
where the time goes in v4:
time: 78.1 us; the launch traced here: 77.9 us
  Pallas kernels  75.2 us (96%)
  other arithmetic  1.46 us (2%)
    pallas_call x1, Pallas kernels, shards(): pl.pallas_call(functools.partial(kernel, pa), out_shape=(jax.ShapeDtypeSt...  75.2 us

profile of v4, /device:TPU:32, one launch (start us, length us, event | category | flops | bytes accessed | tf_op | source)
XLA Modules:
  0.0 77.9 jit_solution(14460902880814432041)
XLA Ops:
  0.6 0.0 copy-start
  0.6 75.2 %shard_map.86 = (f32[16,1024]{1,0:T(8,128)}, f32[1,128]{1,0:T(1,128)}) custom-call(bf16[16,1024]{1,0:T(8,128)(2,1)} %prev_hbm.1, s32[16]{0:T(128)} %owner_ref.1, f32[1,1024]{1,0:T(1,128)} %bitcast.4, bf16[448,1024]{1,0:T(8,128)(2,1)} %wg_ref.1, bf16[448,1024]{1,0:T(8,128)(2,1)} %wu_ref.1, bf16[448,1024]{1,0:T(8,128)(2,1)} %wd_ref.1, f32[1,1024]{1,0:T(1,128)} %bitcast.5), custom_call_target="tpu_custom_call" | custom-call | tf_op jit(solution)/shard_map/pallas_call | solution.py:370
  75.9 0.0 copy-done
  75.9 0.0 copy-start.1
  75.9 1.5 %add_convert_fusion = bf16[16,1024]{1,0:T(8,128)(2,1)} fusion(f32[16,1024]{1,0:T(8,128)} %get-tuple-element.4, bf16[16,1024]{1,0:T(8,128)(2,1)S(1)} %copy-done), kind=kLoop, calls=%fused_computation | loop fusion | flops 49152 | bytes 131072 | tf_op jit(solution)/shard_map/convert_element_type | solution.py:409
  77.4 0.0 copy-done.1
  77.4 0.5 slice_bitcast_fusion
Async XLA Ops:
  0.6 75.3 %copy-start = (bf16[16,1024]{1,0:T(8,128)(2,1)S(1)}, bf16[16,1024]{1,0:T(8,128)(2,1)}, u32[]{:S(2)}) copy-start(bf16[16,1024]{1,0:T(8,128)(2,1)} %prev_hbm.1) | copy-start | bytes 98308
  75.9 1.5 %copy-start.1 = (f32[1,128]{1,0:T(1,128)S(1)}, f32[1,128]{1,0:T(1,128)}, u32[]{:S(2)}) copy-start(f32[1,128]{1,0:T(1,128)} %get-tuple-element.5) | copy-start | bytes 1540

commit v5 on v4

--- a/solution.py
+++ b/solution.py
@@ -64,17 +64,20 @@
         return (((yy + dy + NY) % NY) * NZ + (zz + dz + NZ) % NZ, ((xx + dx) % NX) * 2 + core)
 
     used = [0]
+    kinds = {}
     flying = []
 
-    def send(items, union):
+    def send(items, union, kind=None):
         i = used[0]
         used[0] += 1
+        k = kinds.setdefault(kind or i, len(kinds))
         for src, dst, to in items:
-            pltpu.make_async_remote_copy(src_ref=src, dst_ref=dst, send_sem=ssem.at[i], recv_sem=rsem.at[i],
+            pltpu.make_async_remote_copy(src_ref=src, dst_ref=dst, send_sem=ssem.at[k], recv_sem=rsem.at[i],
                                          device_id=to, device_id_type=MESH).start()
-        whole = pltpu.make_async_remote_copy(src_ref=union, dst_ref=union, send_sem=ssem.at[i], recv_sem=rsem.at[i],
+        whole = pltpu.make_async_remote_copy(src_ref=union, dst_ref=union, send_sem=ssem.at[k], recv_sem=rsem.at[i],
                                              device_id=items[0][2], device_id_type=MESH)
-        flying.append(whole)
+        if kind is None:
+            flying.append(whole)
         return whole
 
     tp_peers = [dev(dx=dx, other=o) for dx in range(NX) for o in (False, True) if (dx, o) != (0, False)]
@@ -126,15 +129,15 @@
 
     def spread(w):
         got["p2", w] = send([(x.at[w, 0, 0, :, A], x.at[w, 0, j, :, A], dev(dy=-side[j])) for j in (1, 2, 3)],
-                            x.at[w, 0, pl.ds(1, 3), :, A])
+                            x.at[w, 0, pl.ds(1, 3), :, A], "p2")
         got["q2", w] = send([(x.at[w, 0, 0, :, B], x.at[w, n, 0, :, B], dev(dz=-near[n])) for n in (1, 2, 3)],
-                            x.at[w, pl.ds(1, 3), 0, :, B])
+                            x.at[w, pl.ds(1, 3), 0, :, B], "q2")
 
     for w in range(NW):
         if w:
             @task(f"far{w}")
             def _(w=w):
-                got["far", w] = send([(x.at[0, 0, 0], x.at[w, 0, 0], dev(dz=-FAR[w]))], x.at[w, 0, 0])
+                got["far", w] = send([(x.at[0, 0, 0], x.at[w, 0, 0], dev(dz=-FAR[w]))], x.at[w, 0, 0], "far")
 
         @task(f"s{w}")
         def _(w=w):
@@ -146,13 +149,13 @@
         def _(w=w):
             got["p2", w].wait_recv()
             got["p3", w] = send([(x.at[w, 0, :, :, A], x.at[w, n, :, :, A], dev(dz=-near[n])) for n in (1, 2, 3)],
-                                x.at[w, pl.ds(1, 3), :, :, A])
+                                x.at[w, pl.ds(1, 3), :, :, A], "p3")
 
         @task(f"q{w}")
         def _(w=w):
             got["q2", w].wait_recv()
             got["q3", w] = send([(x.at[w, :, 0, :, B], x.at[w, :, j, :, B], dev(dy=-side[j])) for j in (1, 2, 3)],
-                                x.at[w, :, pl.ds(1, 3), :, B])
+                                x.at[w, :, pl.ds(1, 3), :, B], "q3")
 
     @task("nq")
     def _():
@@ -214,7 +217,7 @@
             got["p3", w].wait_recv()
             got["q3", w].wait_recv()
             gus[w] = product(w, 1 - cc).astype(BF)
-            got["c1", w] = send([(gus.at[w], rc.at[w], dev(other=True))], rc.at[w])
+            got["c1", w] = send([(gus.at[w], rc.at[w], dev(other=True))], rc.at[w], "c1")
             guo[w] = product(w, cc).reshape(NX, blk, width)
 
         @task(f"x{w}")
@@ -223,7 +226,7 @@
             total = guo[w] + rc[w].astype(F32).reshape(NX, blk, width)
             guo[w] = total
             gub[w] = total.astype(BF)
-            got["x", w] = send([(gub.at[w, (xx + dx) % NX], rx.at[w, dx - 1], dev(dx=dx)) for dx in (2, 1, 3)], rx.at[w])
+            got["x", w] = send([(gub.at[w, (xx + dx) % NX], rx.at[w, dx - 1], dev(dx=dx)) for dx in (2, 1, 3)], rx.at[w], "x")
 
         @task(f"h{w}")
         def _(w=w):
@@ -248,12 +251,12 @@
                 value = act(last, pltpu.roll(last, 128 - rest, 1))
                 hid[w, cc, xx, :, pl.ds(full, 128)] = jnp.where(at_lane < rest, value, jnp.zeros_like(value))
             done = hid.at[w, cc, xx]
-            got["h", w] = send([(done, done, dev(dx=dx)) for dx in (2, 1, 3)], hid.at[w, cc, pl.ds(0, NX - 1)])
+            got["h", w] = send([(done, done, dev(dx=dx)) for dx in (2, 1, 3)], hid.at[w, cc, pl.ds(0, NX - 1)], "h")
 
         @task(f"c{w}")
         def _(w=w):
             got["h", w].wait_recv()
-            got["c2", w] = send([(hid.at[w, cc], hid.at[w, cc], dev(other=True))], hid.at[w, cc])
+            got["c2", w] = send([(hid.at[w, cc], hid.at[w, cc], dev(other=True))], hid.at[w, cc], "c2")
 
         @task(f"d{w}")
         def _(w=w):
@@ -261,8 +264,8 @@
             act = hid[w].reshape(2 * half, hpad)
             down = jnp.dot(act, wd[...], preferred_element_type=F32)
             pt[w] = down.astype(BF).reshape(4, NY, rows, feats)
-            got["r1p", w] = send([(pt.at[w, n, :, :, A], r1p.at[w, n - 1], dev(dz=near[n])) for n in (1, 2, 3)], r1p.at[w])
-            got["r1q", w] = send([(pt.at[w, :, j, :, B], r1q.at[w, j - 1], dev(dy=side[j])) for j in (1, 2, 3)], r1q.at[w])
+            got["r1p", w] = send([(pt.at[w, n, :, :, A], r1p.at[w, n - 1], dev(dz=near[n])) for n in (1, 2, 3)], r1p.at[w], "r1p")
+            got["r1q", w] = send([(pt.at[w, :, j, :, B], r1q.at[w, j - 1], dev(dy=side[j])) for j in (1, 2, 3)], r1q.at[w], "r1q")
             v = lax.dot_general(vv[...], act, NT, preferred_element_type=F32)
             rsc[w] = v[0:8]
 
@@ -273,7 +276,7 @@
             for i in range(3):
                 v = v + r1p[w, i].astype(F32)
             pt[w, 0, :, :, A] = v.astype(BF)
-            got["r2p", w] = send([(pt.at[w, 0, j, :, A], r2p.at[w, j - 1], dev(dy=side[j])) for j in (1, 2, 3)], r2p.at[w])
+            got["r2p", w] = send([(pt.at[w, 0, j, :, A], r2p.at[w, j - 1], dev(dy=side[j])) for j in (1, 2, 3)], r2p.at[w], "r2p")
 
         @task(f"f{w}")
         def _(w=w):
@@ -282,7 +285,7 @@
             for i in range(3):
                 v = v + r1q[w, i].astype(F32)
             pt[w, :, 0, :, B] = v.astype(BF)
-            got["r2q", w] = send([(pt.at[w, n, 0, :, B], r2q.at[w, n - 1], dev(dz=near[n])) for n in (1, 2, 3)], r2q.at[w])
+            got["r2q", w] = send([(pt.at[w, n, 0, :, B], r2q.at[w, n - 1], dev(dz=near[n])) for n in (1, 2, 3)], r2q.at[w], "r2q")
 
         @task(f"g{w}")
         def _(w=w):
@@ -294,7 +297,7 @@
             fs[w, :, A] = a.astype(BF)
             fs[w, :, B] = b.astype(BF)
             if w:
-                got["rf", w] = send([(fs.at[w], rf.at[w - 1], dev(dz=FAR[w]))], rf.at[w - 1])
+                got["rf", w] = send([(fs.at[w], rf.at[w - 1], dev(dz=FAR[w]))], rf.at[w - 1], "rf")
 
     bases = (0, len(tp_peers) + 1, len(tp_peers) + len(y_peers) + 2)
 
@@ -351,10 +354,20 @@
         got["rf", w].wait_recv()
         v = v + rf[w - 1].astype(F32)
     out_ref[...] = v
-    assert used[0] == ssem.shape[0]
+    assert (used[0], len(kinds)) == (rsem.shape[0], ssem.shape[0])
     score_ref[...] = collect("s3", bases[2], z_peers) / keep["count"]
     for copy in flying:
         copy.wait_send()
+    later = pl.ds(1, NW - 1)
+    every = {
+        "far": x.at[later, 0, 0], "p2": x.at[:, 0, pl.ds(1, 3), :, A], "q2": x.at[:, pl.ds(1, 3), 0, :, B],
+        "p3": x.at[:, pl.ds(1, 3), :, :, A], "q3": x.at[:, :, pl.ds(1, 3), :, B], "c1": rc, "x": rx,
+        "h": hid.at[:, cc, pl.ds(0, NX - 1)], "c2": hid.at[:, cc], "r1p": r1p, "r1q": r1q, "r2p": r2p, "r2q": r2q,
+        "rf": rf,
+    }
+    for kind, union in every.items():
+        pltpu.make_async_remote_copy(src_ref=union, dst_ref=union, send_sem=ssem.at[kinds[kind]], recv_sem=rsem.at[0],
+                                     device_id=tp_peers[0], device_id_type=MESH).wait_send()
 
 
 def shards(preview, row_owner, norm_gain, w_gate, w_up, w_down, score_vec):
@@ -364,7 +377,7 @@
     half, blk, wide = 2 * NY * rows, 2 * NY * rows // NX, 2 * hidden
     pa = feats // 256 * 128
     pb = feats - pa
-    sems = 61
+    sems, kinds = 61, 21
     vmem = pl.BlockSpec(memory_space=pltpu.VMEM)
     hbm = pl.BlockSpec(memory_space=pl.ANY)
     verified, scores = pl.pallas_call(
@@ -400,7 +413,7 @@
             pltpu.VMEM((NW, 8, 2 * half), F32),
             pltpu.VMEM((2 * NX + NY + NZ, 1, 128), F32),
             pltpu.SemaphoreType.DMA((8,)),
-            pltpu.SemaphoreType.DMA((sems,)),
+            pltpu.SemaphoreType.DMA((kinds,)),
             pltpu.SemaphoreType.DMA((sems,)),
         ],
         compiler_params=pltpu.CompilerParams(

time: 78.1 us -> 77.7 us (level)
  no operation moved by 1% of the time
where the time goes in v5:
time: 77.7 us; the launch traced here: 77.5 us
  Pallas kernels  74.8 us (96%)
  other arithmetic  1.46 us (2%)
    pallas_call x1, Pallas kernels, shards(): pl.pallas_call(functools.partial(kernel, pa), out_shape=(jax.ShapeDtypeSt...  74.8 us

profile of v5, /device:TPU:32, one launch (start us, length us, event | category | flops | bytes accessed | tf_op | source)
XLA Modules:
  0.0 77.5 jit_solution(16313337471385256278)
XLA Ops:
  0.6 0.0 copy-start
  0.6 74.8 %shard_map.86 = (f32[16,1024]{1,0:T(8,128)}, f32[1,128]{1,0:T(1,128)}) custom-call(bf16[16,1024]{1,0:T(8,128)(2,1)} %prev_hbm.1, s32[16]{0:T(128)} %owner_ref.1, f32[1,1024]{1,0:T(1,128)} %bitcast.4, bf16[448,1024]{1,0:T(8,128)(2,1)} %wg_ref.1, bf16[448,1024]{1,0:T(8,128)(2,1)} %wu_ref.1, bf16[448,1024]{1,0:T(8,128)(2,1)} %wd_ref.1, f32[1,1024]{1,0:T(1,128)} %bitcast.5), custom_call_target="tpu_custom_call" | custom-call | tf_op jit(solution)/shard_map/pallas_call | solution.py:383
  75.5 0.0 copy-done
  75.5 0.0 copy-start.1
  75.5 1.5 %add_convert_fusion = bf16[16,1024]{1,0:T(8,128)(2,1)} fusion(f32[16,1024]{1,0:T(8,128)} %get-tuple-element.4, bf16[16,1024]{1,0:T(8,128)(2,1)S(1)} %copy-done), kind=kLoop, calls=%fused_computation | loop fusion | flops 49152 | bytes 131072 | tf_op jit(solution)/shard_map/convert_element_type | solution.py:422
  76.9 0.0 copy-done.1
  77.0 0.5 slice_bitcast_fusion
Async XLA Ops:
  0.6 74.8 %copy-start = (bf16[16,1024]{1,0:T(8,128)(2,1)S(1)}, bf16[16,1024]{1,0:T(8,128)(2,1)}, u32[]{:S(2)}) copy-start(bf16[16,1024]{1,0:T(8,128)(2,1)} %prev_hbm.1) | copy-start | bytes 98308
  75.5 1.5 %copy-start.1 = (f32[1,128]{1,0:T(1,128)S(1)}, f32[1,128]{1,0:T(1,128)}, u32[]{:S(2)}) copy-start(f32[1,128]{1,0:T(1,128)} %get-tuple-element.5) | copy-start | bytes 1540

commit v6 on v5

--- a/solution.py
+++ b/solution.py
@@ -116,7 +116,6 @@
     eye = (lax.broadcasted_iota(jnp.int32, (rows, 128), 1) % rows
            == lax.broadcasted_iota(jnp.int32, (rows, 128), 0))
     nq[0] = jnp.sum(jnp.where(eye, sq, 0.0), axis=0, keepdims=True)
-    pl.semaphore_wait(barrier, len(tp_peers + y_peers + z_peers))
 
     got = {}
     tasks = {}
@@ -346,8 +345,13 @@
         exchange("s3", bases[2], collect("s2", bases[1], y_peers), z_peers)
 
     assert sorted(ORDER) == sorted(tasks)
+    early = ("wts", "vec")
+    for name in early:
+        tasks[name]()
+    pl.semaphore_wait(barrier, len(tp_peers + y_peers + z_peers))
     for name in ORDER:
-        tasks[name]()
+        if name not in early:
+            tasks[name]()
 
     v = fs[0].astype(F32)
     for w in range(1, NW):

time: 77.7 us -> 78.4 us (level)
  the two profiles are of different devices: /device:TPU:32 before, /device:TPU:1 now
where the time goes in v6:
time: 78.4 us; the launch traced here: 78.1 us
  Pallas kernels  75.5 us (96%)
  other arithmetic  1.46 us (2%)
    pallas_call x1, Pallas kernels, shards(): pl.pallas_call(functools.partial(kernel, pa), out_shape=(jax.ShapeDtypeSt...  75.5 us

profile of v6, /device:TPU:1, one launch (start us, length us, event | category | flops | bytes accessed | tf_op | source)
XLA Modules:
  0.0 78.1 jit_solution(4045976898575667244)
XLA Ops:
  0.6 0.0 copy-start
  0.6 75.5 %shard_map.86 = (f32[16,1024]{1,0:T(8,128)}, f32[1,128]{1,0:T(1,128)}) custom-call(bf16[16,1024]{1,0:T(8,128)(2,1)} %prev_hbm.1, s32[16]{0:T(128)} %owner_ref.1, f32[1,1024]{1,0:T(1,128)} %bitcast.4, bf16[448,1024]{1,0:T(8,128)(2,1)} %wg_ref.1, bf16[448,1024]{1,0:T(8,128)(2,1)} %wu_ref.1, bf16[448,1024]{1,0:T(8,128)(2,1)} %wd_ref.1, f32[1,1024]{1,0:T(1,128)} %bitcast.5), custom_call_target="tpu_custom_call" | custom-call | tf_op jit(solution)/shard_map/pallas_call | solution.py:387
  76.2 0.0 copy-done
  76.2 0.0 copy-start.1
  76.2 1.5 %add_convert_fusion = bf16[16,1024]{1,0:T(8,128)(2,1)} fusion(f32[16,1024]{1,0:T(8,128)} %get-tuple-element.4, bf16[16,1024]{1,0:T(8,128)(2,1)S(1)} %copy-done), kind=kLoop, calls=%fused_computation | loop fusion | flops 49152 | bytes 131072 | tf_op jit(solution)/shard_map/convert_element_type | solution.py:426
  77.6 0.0 copy-done.1
  77.6 0.5 slice_bitcast_fusion
Async XLA Ops:
  0.6 75.5 %copy-start = (bf16[16,1024]{1,0:T(8,128)(2,1)S(1)}, bf16[16,1024]{1,0:T(8,128)(2,1)}, u32[]{:S(2)}) copy-start(bf16[16,1024]{1,0:T(8,128)(2,1)} %prev_hbm.1) | copy-start | bytes 98308
  76.2 1.5 %copy-start.1 = (f32[1,128]{1,0:T(1,128)S(1)}, f32[1,128]{1,0:T(1,128)}, u32[]{:S(2)}) copy-start(f32[1,128]{1,0:T(1,128)} %get-tuple-element.5) | copy-start | bytes 1540
